TPU v7x, 512 devices: a whole 4x8x8 slice. The times are simulated.
512 devices in a mesh: chan: 32 (over z, y_lo), win: 16 (over x, y_hi, core).
Axes of the slice: x: 4, y: 8 (y_hi: 2, y_lo: 4; y = y_hi * 4 + y_lo), z: 8, core: 2. Of those that a mesh axis runs over, the one named last changes fastest.
Arguments:
- spectra: bfloat16 [16, 4096, 1536], P('win', 'chan'), may hold values from -120 to 120
- masks: int32 [16, 4096], replicated, may hold values from 0 to 1, as said below
- matching: int32 [2, 32], replicated, may hold values from 0 to 31, as said below
Outputs:
- corr: bfloat16 [2, 4096, 8192], P(None, ('chan', 'win'))
Inputs may be any that keep to these rules, and one draw needn't show every extreme that they name: `masks`: some channels are 0 in every window. `matching`: in round r every block i meets block i XOR s_r, with one s_r for each round, and each bit of 31 is set in exactly one of the two rounds' s_r.
All inputs are finite; a program needn't handle non-finite values.
Results may differ from a plain program's by a relative error of at most 0.014.
Values may be sent and summed in bfloat16 or wider, within the bound.
A program may use at most 64 MiB of HBM per device.

v0:
```python
import math

import jax
import jax.numpy as jnp
from jax import lax
from jax.sharding import PartitionSpec as P

LAGS = 64
ROUNDS = 2


def partner_2(value, axis, apart):
    mask = 2**apart
    pairs = [(source, source ^ mask) for source in range(lax.axis_size(axis))]
    return lax.ppermute(value, axis, pairs)


def scattered(product, extent, axis):
    everything = product(jnp.int32(0), lax.axis_size(axis) * extent)
    own = lax.psum_scatter(everything.astype(jnp.bfloat16), axis, scatter_dimension=0, tiled=True)
    return own.astype(jnp.float32)


def tables(bin_count, lag_count):
    freq = jnp.arange(bin_count, dtype=jnp.int32)
    lag_ids = jnp.arange(lag_count, dtype=jnp.int32)
    phase = lag_ids[:, None] * freq[None, :] % (2 * bin_count)
    angle = phase.astype(jnp.float32) * (math.pi / bin_count)
    return (jnp.cos(angle), jnp.sin(angle))


def rotate(own_rows, cosine, sine):
    bin_count = cosine.shape[1]
    real_part = own_rows[..., :bin_count].astype(jnp.float32)[:, :, None, :]
    imag_part = own_rows[..., bin_count:].astype(jnp.float32)[:, :, None, :]
    turned = jnp.concatenate(
        [real_part * cosine - imag_part * sine, real_part * sine + imag_part * cosine], axis=-1
    )
    turned = turned.astype(jnp.bfloat16)
    return turned.reshape(own_rows.shape[0], own_rows.shape[1] * cosine.shape[0], 2 * bin_count)


def whiten(spectra, flags):
    values = spectra.astype(jnp.float32)
    mean_square = jnp.mean(values * values, axis=-1, keepdims=True)
    return (flags.astype(jnp.float32)[..., None] * values * lax.rsqrt(mean_square + 1e-06)).astype(
        jnp.bfloat16
    )


def deliver(values, flip_bits):
    levels = lax.axis_size("chan").bit_length() - 1
    for bit_number in range(levels):
        moved = partner_2(values, "chan", bit_number)
        taken = jnp.right_shift(flip_bits, bit_number) & 1 == 1
        values = jnp.where(taken, moved, values)
    return values


def rows_term(row_total, whitened, partner_list, cosine, sine):
    row_step = math.gcd(row_total, 8)
    block_rows = whitened.shape[1]

    def one_piece(piece_id):
        own_rows = lax.dynamic_slice_in_dim(whitened, piece_id * row_step, row_step, 1)
        rotated = rotate(own_rows, cosine, sine)
        results = []
        for other_spec in partner_list:
            term = lax.dot_general(
                rotated,
                other_spec,
                (((0, 2), (0, 2)), ((), ())),
                preferred_element_type=jnp.float32,
            )
            results.append(term.reshape(row_step, LAGS * block_rows))
        return jnp.concatenate(results, axis=1)

    pieces = lax.map(one_piece, jnp.arange(row_total // row_step, dtype=jnp.int32))
    return pieces.reshape(row_total, pieces.shape[2])


def shards(spectra, masks, matching):
    block_id = lax.axis_index("chan")
    slot_id = lax.axis_index("win")
    win_count = lax.axis_size("win")
    w_count, block_rows, two_bins = spectra.shape
    bin_count = two_bins // 2
    row_count = block_rows // win_count
    own_flags = lax.dynamic_slice(
        masks, (slot_id * w_count, block_id * block_rows), (w_count, block_rows)
    )
    whitened = whiten(spectra, own_flags)
    cosine, sine = tables(bin_count, LAGS)
    flags = masks.astype(jnp.bfloat16)
    own_cols = lax.dynamic_slice_in_dim(flags, block_id * block_rows, block_rows, 1)
    count_list = []
    for round_id in range(ROUNDS):
        partner = matching[round_id, block_id]
        other_cols = lax.dynamic_slice_in_dim(flags, partner * block_rows, block_rows, 1)
        count_list.append(
            lax.dot_general(
                own_cols, other_cols, (((0,), (0,)), ((), ())), preferred_element_type=jnp.float32
            )
        )
    partner_list = []
    for round_id in range(ROUNDS):
        partner_list.append(
            deliver(whitened, jnp.bitwise_xor(matching[round_id, block_id], block_id))
        )
    stacked_list = []
    for round_id in range(ROUNDS):
        chosen = [partner_list[round_id]]
        stacked_list.append(
            scattered(
                lambda first_row, row_total, chosen=chosen: rows_term(
                    row_total, whitened, chosen, cosine, sine
                ),
                row_count,
                "win",
            )
        )
    outputs = []
    for round_id in range(ROUNDS):
        counts = lax.dynamic_slice_in_dim(count_list[round_id], slot_id * row_count, row_count, 0)
        scale = jnp.sqrt(bin_count * jnp.maximum(counts, 1.0))
        shaped = stacked_list[round_id].reshape(row_count, LAGS, block_rows) / scale[:, None, :]
        outputs.append(shaped.reshape(row_count, LAGS * block_rows).astype(jnp.bfloat16))
    return jnp.stack(outputs, axis=0)


def solution(mesh):
    in_specs = (P("win", "chan", None), P(), P())
    out_specs = P(None, ("chan", "win"), None)
    return jax.shard_map(shards, mesh=mesh, in_specs=in_specs, out_specs=out_specs, check_vma=False)
```

profile of v0, /device:TPU:6, one launch (start us, length us, event | category | flops | bytes accessed | tf_op | source)
XLA Modules:
  0.0 391.9 jit_solution(9002293265614346454)
XLA Ops:
  6.5 1.2 fusion.40
  8.5 1.2 fusion.39
  9.7 3.5 collective-permute-start
  13.2 1.4 constant_dynamic-slice_fusion
  15.9 6.5 %collective-permute-done = bf16[1,128,1536]{2,1,0:T(8,128)(2,1)S(1)} collective-permute-done((bf16[1,128,1536]{2,1,0:T(8,128)(2,1)S(1)}, bf16[1,128,1536]{2,1,0:T(8,128)(2,1)S(1)}, u32[]{:S(2)}, u32[]{:S(2)}) %collective-permute-start) | collective-permute-done | bytes 393248 | tf_op jit(solution)/shard_map/ppermute | solution.py:15
  22.5 1.3 broadcast_select_fusion.5
  23.8 4.5 %collective-permute-start.1 = (bf16[1,128,1536]{2,1,0:T(8,128)(2,1)S(1)}, bf16[1,128,1536]{2,1,0:T(8,128)(2,1)S(1)}, u32[]{:S(2)}, u32[]{:S(2)}) collective-permute-start(bf16[1,128,1536]{2,1,0:T(8,128)(2,1)S(1)} %get-tuple-element.193), channel_id=1, source_target_pairs={{0,32},{16,48},{32,0},{48,16},{64,96},{80,112},{96,64},{112,80},{1... | collective-permute-start | bytes 1179656 | tf_op jit(solution)/shard_map/ppermute | solution.py:15
  28.3 2.2 collective-permute-start.5
  30.6 24.0 %collective-permute-done.1 = bf16[1,128,1536]{2,1,0:T(8,128)(2,1)S(1)} collective-permute-done((bf16[1,128,1536]{2,1,0:T(8,128)(2,1)S(1)}, bf16[1,128,1536]{2,1,0:T(8,128)(2,1)S(1)}, u32[]{:S(2)}, u32[]{:S(2)}) %collective-permute-start.1) | collective-permute-done | bytes 393248 | tf_op jit(solution)/shard_map/ppermute | solution.py:15
  54.6 4.3 %collective-permute-start.2 = (bf16[1,128,1536]{2,1,0:T(8,128)(2,1)S(1)}, bf16[1,128,1536]{2,1,0:T(8,128)(2,1)S(1)}, u32[]{:S(2)}, u32[]{:S(2)}) collective-permute-start(bf16[1,128,1536]{2,1,0:T(8,128)(2,1)S(1)} %broadcast_select_fusion.6), channel_id=1, source_target_pairs={{0,64},{16,80},{32,96},{48,112},{64,0},{80,16},{96,32},{112,48},{1... | collective-permute-start | bytes 1179656 | tf_op jit(solution)/shard_map/ppermute | solution.py:15
  58.9 3.0 collective-permute-done.5
  61.9 4.3 %collective-permute-start.6 = (bf16[1,128,1536]{2,1,0:T(8,128)(2,1)S(1)}, bf16[1,128,1536]{2,1,0:T(8,128)(2,1)S(1)}, u32[]{:S(2)}, u32[]{:S(2)}) collective-permute-start(bf16[1,128,1536]{2,1,0:T(8,128)(2,1)S(1)} %broadcast_select_fusion.1), channel_id=1, source_target_pairs={{0,64},{16,80},{32,96},{48,112},{64,0},{80,16},{96,32},{112,48},{1... | collective-permute-start | bytes 1179656 | tf_op jit(solution)/shard_map/ppermute | solution.py:15
  66.3 6.1 %collective-permute-start.3 = (bf16[1,128,1536]{2,1,0:T(8,128)(2,1)S(1)}, bf16[1,128,1536]{2,1,0:T(8,128)(2,1)S(1)}, u32[]{:S(2)}, u32[]{:S(2)}) collective-permute-start(bf16[1,128,1536]{2,1,0:T(8,128)(2,1)S(1)} %broadcast_select_fusion.7), channel_id=1, source_target_pairs={{0,128},{16,144},{32,160},{48,176},{64,192},{80,208},{96,224},{112... | collective-permute-start | bytes 1179656 | tf_op jit(solution)/shard_map/ppermute | solution.py:15
  72.4 8.3 %collective-permute-done.6 = bf16[1,128,1536]{2,1,0:T(8,128)(2,1)S(1)} collective-permute-done((bf16[1,128,1536]{2,1,0:T(8,128)(2,1)S(1)}, bf16[1,128,1536]{2,1,0:T(8,128)(2,1)S(1)}, u32[]{:S(2)}, u32[]{:S(2)}) %collective-permute-start.6) | collective-permute-done | bytes 393248 | tf_op jit(solution)/shard_map/ppermute | solution.py:15
  80.7 2.9 collective-permute-start.7
  83.6 15.5 %collective-permute-done.3 = bf16[1,128,1536]{2,1,0:T(8,128)(2,1)S(1)} collective-permute-done((bf16[1,128,1536]{2,1,0:T(8,128)(2,1)S(1)}, bf16[1,128,1536]{2,1,0:T(8,128)(2,1)S(1)}, u32[]{:S(2)}, u32[]{:S(2)}) %collective-permute-start.3) | collective-permute-done | bytes 393248 | tf_op jit(solution)/shard_map/ppermute | solution.py:15
  99.2 8.8 %collective-permute-start.4 = (bf16[1,128,1536]{2,1,0:T(8,128)(2,1)S(1)}, bf16[1,128,1536]{2,1,0:T(8,128)(2,1)S(1)}, u32[]{:S(2)}, u32[]{:S(2)}) collective-permute-start(bf16[1,128,1536]{2,1,0:T(8,128)(2,1)S(1)} %broadcast_select_fusion.8), channel_id=1, source_target_pairs={{0,256},{16,272},{32,288},{48,304},{64,320},{80,336},{96,352},{112... | collective-permute-start | bytes 1179656 | tf_op jit(solution)/shard_map/ppermute | solution.py:15
  108.0 2.1 collective-permute-done.7
  110.1 12.6 %collective-permute-start.8 = (bf16[1,128,1536]{2,1,0:T(8,128)(2,1)S(1)}, bf16[1,128,1536]{2,1,0:T(8,128)(2,1)S(1)}, u32[]{:S(2)}, u32[]{:S(2)}) collective-permute-start(bf16[1,128,1536]{2,1,0:T(8,128)(2,1)S(1)} %broadcast_select_fusion.3), channel_id=1, source_target_pairs={{0,256},{16,272},{32,288},{48,304},{64,320},{80,336},{96,352},{112... | collective-permute-start | bytes 1179656 | tf_op jit(solution)/shard_map/ppermute | solution.py:15
  123.7 49.0 %while.24 = (s32[]{:T(128)}, bf16[16,8,8192]{2,1,0:T(8,128)(2,1)S(1)}, s32[16]{0:T(128)S(1)}, bf16[1,128,1536]{2,1,0:T(8,128)(2,1)S(1)}, bf16[1,128,1536]{2,1,0:...) while((s32[]{:T(128)}, ...), condition=%wide.region_2.3_spmd.clone.clone, body=%wide.region_1.2_spmd.clone.clone.sunk | while | flops 208072704 | bytes 6676691 | solution.py:78
  127.9 0.8 fusion.65
  137.1 0.8 fusion.65
  143.2 0.8 fusion.65
  152.4 0.8 fusion.65
  155.5 0.8 fusion.65
  172.7 1.3 copy-done.1
  175.9 49.3 %while.25 = (s32[]{:T(128)}, bf16[16,8,8192]{2,1,0:T(8,128)(2,1)S(1)}, s32[16]{0:T(128)S(1)}, bf16[1,128,1536]{2,1,0:T(8,128)(2,1)S(1)}, bf16[1,128,1536]{2,1,0:...) while((s32[]{:T(128)}, ...), condition=%wide.region_5.6_spmd.clone.clone, body=%wide.region_4.5_spmd.clone.clone.sunk | while | flops 208072704 | bytes 5103799 | solution.py:78
  225.2 1.3 copy-done
  228.3 58.4 %reduce-scatter.3.cloned.1.call-done = bf16[8,8192]{1,0:T(8,128)(2,1)} async-done(((bf16[128,8192]{1,0:T(8,128)(2,1)}), bf16[8,8192]{1,0:T(8,128)(2,1)}) %reduce-scatter.3.cloned.1.call-update) | async-done | bytes 131088 | tf_op jit(solution)/shard_map/reduce_scatter | solution.py:20
  286.7 0.9 fusion.43
  287.6 95.8 %reduce-scatter.5.cloned.1.call-done = bf16[8,8192]{1,0:T(8,128)(2,1)} async-done(((bf16[128,8192]{1,0:T(8,128)(2,1)}), bf16[8,8192]{1,0:T(8,128)(2,1)}) %reduce-scatter.5.cloned.1.call-update) | async-done | bytes 131088 | tf_op jit(solution)/shard_map/reduce_scatter | solution.py:20
  383.4 0.9 fusion.44
  (283 shorter events, 79.4 us)
Async XLA Ops:
  6.5 280.2 %reduce-scatter.3.cloned.1.call-start = ((), (), s32[]{:S(2)}) async-start(), calls=%async_computation.2 | async-start | bytes 2228224 | tf_op jit(solution)/shard_map/reduce_scatter | solution.py:20
  9.7 12.7 %collective-permute-start = (bf16[1,128,1536]{2,1,0:T(8,128)(2,1)S(1)}, bf16[1,128,1536]{2,1,0:T(8,128)(2,1)S(1)}, u32[]{:S(2)}, u32[]{:S(2)}) collective-permute-start(bf16[1,128,1536]{2,1,0:T(8,128)(2,1)S(1)} %fusion.39), channel_id=1, source_target_pairs={{0,16},{16,0},{32,48},{48,32},{64,80},{80,64},{96,112},{112,96},{1... | collective-permute-start | bytes 1179656 | tf_op jit(solution)/shard_map/ppermute | solution.py:15
  23.8 30.8 %collective-permute-start.1 = (bf16[1,128,1536]{2,1,0:T(8,128)(2,1)S(1)}, bf16[1,128,1536]{2,1,0:T(8,128)(2,1)S(1)}, u32[]{:S(2)}, u32[]{:S(2)}) collective-permute-start(bf16[1,128,1536]{2,1,0:T(8,128)(2,1)S(1)} %get-tuple-element.193), channel_id=1, source_target_pairs={{0,32},{16,48},{32,0},{48,16},{64,96},{80,112},{96,64},{112,80},{1... | collective-permute-start | bytes 1179656 | tf_op jit(solution)/shard_map/ppermute | solution.py:15
  28.3 33.5 %collective-permute-start.5 = (bf16[1,128,1536]{2,1,0:T(8,128)(2,1)S(1)}, bf16[1,128,1536]{2,1,0:T(8,128)(2,1)S(1)}, u32[]{:S(2)}, u32[]{:S(2)}) collective-permute-start(bf16[1,128,1536]{2,1,0:T(8,128)(2,1)S(1)} %get-tuple-element.194), channel_id=1, source_target_pairs={{0,32},{16,48},{32,0},{48,16},{64,96},{80,112},{96,64},{112,80},{1... | collective-permute-start | bytes 1179656 | tf_op jit(solution)/shard_map/ppermute | solution.py:15
  54.6 11.6 %collective-permute-start.2 = (bf16[1,128,1536]{2,1,0:T(8,128)(2,1)S(1)}, bf16[1,128,1536]{2,1,0:T(8,128)(2,1)S(1)}, u32[]{:S(2)}, u32[]{:S(2)}) collective-permute-start(bf16[1,128,1536]{2,1,0:T(8,128)(2,1)S(1)} %broadcast_select_fusion.6), channel_id=1, source_target_pairs={{0,64},{16,80},{32,96},{48,112},{64,0},{80,16},{96,32},{112,48},{1... | collective-permute-start | bytes 1179656 | tf_op jit(solution)/shard_map/ppermute | solution.py:15
  61.9 18.8 %collective-permute-start.6 = (bf16[1,128,1536]{2,1,0:T(8,128)(2,1)S(1)}, bf16[1,128,1536]{2,1,0:T(8,128)(2,1)S(1)}, u32[]{:S(2)}, u32[]{:S(2)}) collective-permute-start(bf16[1,128,1536]{2,1,0:T(8,128)(2,1)S(1)} %broadcast_select_fusion.1), channel_id=1, source_target_pairs={{0,64},{16,80},{32,96},{48,112},{64,0},{80,16},{96,32},{112,48},{1... | collective-permute-start | bytes 1179656 | tf_op jit(solution)/shard_map/ppermute | solution.py:15
  66.3 32.9 %collective-permute-start.3 = (bf16[1,128,1536]{2,1,0:T(8,128)(2,1)S(1)}, bf16[1,128,1536]{2,1,0:T(8,128)(2,1)S(1)}, u32[]{:S(2)}, u32[]{:S(2)}) collective-permute-start(bf16[1,128,1536]{2,1,0:T(8,128)(2,1)S(1)} %broadcast_select_fusion.7), channel_id=1, source_target_pairs={{0,128},{16,144},{32,160},{48,176},{64,192},{80,208},{96,224},{112... | collective-permute-start | bytes 1179656 | tf_op jit(solution)/shard_map/ppermute | solution.py:15
  80.7 29.3 %collective-permute-start.7 = (bf16[1,128,1536]{2,1,0:T(8,128)(2,1)S(1)}, bf16[1,128,1536]{2,1,0:T(8,128)(2,1)S(1)}, u32[]{:S(2)}, u32[]{:S(2)}) collective-permute-start(bf16[1,128,1536]{2,1,0:T(8,128)(2,1)S(1)} %broadcast_select_fusion.2), channel_id=1, source_target_pairs={{0,128},{16,144},{32,160},{48,176},{64,192},{80,208},{96,224},{112... | collective-permute-start | bytes 1179656 | tf_op jit(solution)/shard_map/ppermute | solution.py:15
  99.2 23.4 %collective-permute-start.4 = (bf16[1,128,1536]{2,1,0:T(8,128)(2,1)S(1)}, bf16[1,128,1536]{2,1,0:T(8,128)(2,1)S(1)}, u32[]{:S(2)}, u32[]{:S(2)}) collective-permute-start(bf16[1,128,1536]{2,1,0:T(8,128)(2,1)S(1)} %broadcast_select_fusion.8), channel_id=1, source_target_pairs={{0,256},{16,272},{32,288},{48,304},{64,320},{80,336},{96,352},{112... | collective-permute-start | bytes 1179656 | tf_op jit(solution)/shard_map/ppermute | solution.py:15
  110.1 64.0 %collective-permute-start.8 = (bf16[1,128,1536]{2,1,0:T(8,128)(2,1)S(1)}, bf16[1,128,1536]{2,1,0:T(8,128)(2,1)S(1)}, u32[]{:S(2)}, u32[]{:S(2)}) collective-permute-start(bf16[1,128,1536]{2,1,0:T(8,128)(2,1)S(1)} %broadcast_select_fusion.3), channel_id=1, source_target_pairs={{0,256},{16,272},{32,288},{48,304},{64,320},{80,336},{96,352},{112... | collective-permute-start | bytes 1179656 | tf_op jit(solution)/shard_map/ppermute | solution.py:15
  124.8 1.3 copy-start.3
  127.9 1.3 copy-start.3
  130.9 1.3 copy-start.3
  134.0 1.3 copy-start.3
  137.1 1.3 copy-start.3
  140.1 1.3 copy-start.3
  143.2 1.3 copy-start.3
  146.2 1.3 copy-start.3
  149.3 1.3 copy-start.3
  152.4 1.3 copy-start.3
  155.4 1.3 copy-start.3
  158.5 1.3 copy-start.3
  161.6 1.3 copy-start.3
  164.6 1.3 copy-start.3
  167.7 1.3 copy-start.3
  170.8 1.3 copy-start.3
  172.7 1.3 copy-start.1
  174.1 209.4 %reduce-scatter.5.cloned.1.call-start = ((), (), s32[]{:S(2)}) async-start(), calls=%async_computation.3 | async-start | bytes 2228224 | tf_op jit(solution)/shard_map/reduce_scatter | solution.py:20
  174.9 1.0 copy-start.2
  225.2 1.3 copy-start
  225.2 2.0 copy-start.4
Sparse Core Ops, SparseCore 0:
  174.2 112.4 reduce-scatter.2
  291.5 91.8 reduce-scatter.4
where the time goes:
time: 393 us; the launch traced here: 392 us
  waiting for transfers between devices  214 us (54%)
  starting transfers between devices  49.1 us (12%)
  other arithmetic  48.6 us (12%)
  local copies, waits for them, and re-layouts  25.9 us (7%)
  loops' own time  20 us (5%)
  matrix products  18.5 us (5%)
  between operations  16.3 us (4%)
    reduce_scatter x2, waiting for transfers between devices, scattered(): lax.psum_scatter(everything.astype(jnp.bfloat16), axis, scatter_dimension...  154 us
    ppermute x9, waiting for transfers between devices, partner_2(): return lax.ppermute(value, axis, pairs)  59.4 us
    ppermute x9, starting transfers between devices, partner_2(): return lax.ppermute(value, axis, pairs)  49.1 us
    sin x32, other arithmetic, tables(): return (jnp.cos(angle), jnp.sin(angle))  25.8 us
    another operation x2, loops' own time, rows_term(): lax.map(one_piece, jnp.arange(row_total // row_step, dtype=jnp.int32))  20 us
    dynamic_slice x32, local copies, waits for them, and re-layouts, rows_term(): lax.map(one_piece, jnp.arange(row_total // row_step, dtype=jnp.int32))  18.2 us
    dot_general x32, matrix products, one_piece(): lax.dot_general(rotated, other_spec, (((0, 2), (0, 2)), ((), ())), prefer...  18.1 us
    another operation x32, other arithmetic  13.4 us
  transfers between devices with their start and end apart: 11, of which 8 were waited for; matrix products, arithmetic and copies ran while one was open for 21% of the time, Pallas kernels for 0%

commit v1 on v0

v1 whole, which is shorter than its diff:
```python
import functools
import math

import jax
import jax.numpy as jnp
import numpy as np
from jax import lax
from jax.experimental import pallas as pl
from jax.experimental.pallas import tpu as pltpu
from jax.sharding import PartitionSpec as P

LAGS = 64
ROUNDS = 2
FINE = 16
COARSE = LAGS // FINE
MESH = pl.DeviceIdType.MESH

FAR_UP, FAR_DOWN, OWN_UP, OWN_DOWN, SUM_UP, SUM_DOWN, ACROSS = range(7)


def tables(bin_count):
    freq = np.arange(bin_count, dtype=np.int64)
    fine = np.arange(FINE, dtype=np.int64)[:, None]
    coarse = FINE * np.arange(COARSE, dtype=np.int64)[:, None]
    lags = np.concatenate([fine, coarse], axis=0)
    angle = (lags * freq % (2 * bin_count)).astype(np.float64) * (math.pi / bin_count)
    return np.cos(angle).astype(np.float32), np.sin(angle).astype(np.float32)


def stack_kernel(own_ref, part_ref, cos_ref, sin_ref, scale_ref, out_ref, own_rx, part_rx, lhs, rhs,
                 mine, held, sends, gets, pair_send, pair_recv, ssem, rsem):
    chan = lax.axis_index("chan")
    win = lax.axis_index("win")
    x_pos = win // 4
    y_pos = (win // 2) % 2
    core = win % 2
    up = (chan, (win + 4) % 16)
    down = (chan, (win + 12) % 16)
    across = (chan, win + 2 - 4 * y_pos)
    twin = (chan, win + 1 - 2 * core)
    bins = own_ref.shape[1] // 2
    rows = FINE * 8

    barrier = pltpu.get_barrier_semaphore()
    for device in (up, down, across, twin):
        pl.semaphore_signal(barrier, inc=1, device_id=device, device_id_type=MESH)
    pl.semaphore_wait(barrier, 4)

    pair_copies = [
        pltpu.make_async_remote_copy(src, dst, pair_send.at[k], pair_recv.at[k], device_id=twin,
                                     device_id_type=MESH)
        for k, (src, dst) in enumerate(
            [(own_ref, own_rx), (part_ref.at[0], part_rx.at[0]), (part_ref.at[1], part_rx.at[1])])
    ]
    for copy in pair_copies:
        copy.start()

    def rotate_own(src, slot):
        @pl.loop(0, 8)
        def _(group):
            both = src[pl.ds(pl.multiple_of(group * 16, 16), 16), :].astype(jnp.float32)
            own = jnp.where(core == 0, both[:8], both[8:])
            real, imag = own[:, :bins], own[:, bins:]
            for pair in range(FINE // 2):
                reals, imags = [], []
                for lag in (2 * pair, 2 * pair + 1):
                    cosine, sine = cos_ref[lag : lag + 1, :], sin_ref[lag : lag + 1, :]
                    reals.append(real * cosine - imag * sine)
                    imags.append(real * sine + imag * cosine)
                at = pl.ds(pl.multiple_of(group * rows + pair * 16, 16), 16)
                lhs[at, slot * 2 * bins : slot * 2 * bins + bins] = jnp.concatenate(
                    reals, axis=0).astype(jnp.bfloat16)
                lhs[at, slot * 2 * bins + bins : (slot + 1) * 2 * bins] = jnp.concatenate(
                    imags, axis=0).astype(jnp.bfloat16)

    def rotate_other(src, round_id, slot):
        @pl.loop(0, 8)
        def _(group):
            block = src[pl.ds(pl.multiple_of(group * 16, 16), 16), :].astype(jnp.float32)
            real, imag = block[:, :bins], block[:, bins:]
            for lag in range(COARSE):
                cosine = cos_ref[FINE + lag : FINE + lag + 1, :]
                sine = sin_ref[FINE + lag : FINE + lag + 1, :]
                at = pl.ds(
                    pl.multiple_of((round_id * COARSE + lag) * 128 + group * 16, 16), 16)
                rhs[at, slot * 2 * bins : slot * 2 * bins + bins] = (
                    real * cosine + imag * sine).astype(jnp.bfloat16)
                rhs[at, slot * 2 * bins + bins : (slot + 1) * 2 * bins] = (
                    imag * cosine - real * sine).astype(jnp.bfloat16)

    rotate_own(own_ref, 0)
    rotate_other(part_ref.at[0], 0, 0)
    rotate_other(part_ref.at[1], 1, 0)
    pair_copies[0].wait_recv()
    rotate_own(own_rx, 1)
    pair_copies[1].wait_recv()
    rotate_other(part_rx.at[0], 0, 1)
    pair_copies[2].wait_recv()
    rotate_other(part_rx.at[1], 1, 1)

    def copy_of(kind, piece):
        device = (up, down, up, down, up, down, across)[kind]
        return pltpu.make_async_remote_copy(
            sends.at[piece, kind], gets.at[piece, kind], ssem.at[piece, kind],
            rsem.at[piece, kind], device_id=device, device_id_type=MESH)

    def product(piece, x_to):
        left = lhs[pl.ds(pl.multiple_of(x_to * 2 * rows, 2 * rows), 2 * rows), :]
        right = rhs[pl.ds(pl.multiple_of(piece * 256, 256), 256), :]
        return lax.dot_general(left, right, (((1,), (1,)), ((), ())),
                               preferred_element_type=jnp.float32)

    def compute(piece):
        far = product(piece, (x_pos + 2) % 4)
        sends[piece, FAR_UP] = far[:rows].astype(jnp.bfloat16)
        sends[piece, FAR_DOWN] = far[rows:].astype(jnp.bfloat16)
        copy_of(FAR_UP, piece).start()
        copy_of(FAR_DOWN, piece).start()
        near = product(piece, (x_pos + 1) % 4)
        held[piece, 0] = near[:rows]
        sends[piece, OWN_UP] = near[rows:].astype(jnp.bfloat16)
        copy_of(OWN_UP, piece).start()
        near = product(piece, (x_pos + 3) % 4)
        sends[piece, OWN_DOWN] = near[:rows].astype(jnp.bfloat16)
        copy_of(OWN_DOWN, piece).start()
        held[piece, 1] = near[rows:]
        own = product(piece, x_pos)
        mine[piece, 0] = own[:rows]
        mine[piece, 1] = own[rows:]

    def pass_on(piece):
        for kind, far in ((SUM_UP, FAR_UP), (SUM_DOWN, FAR_DOWN)):
            copy_of(far, piece).wait_recv()
            total = held[piece, kind - SUM_UP] + gets[piece, far].astype(jnp.float32)
            sends[piece, kind] = total.astype(jnp.bfloat16)
            copy_of(kind, piece).start()

    def along_x(piece, y_to):
        return (mine[piece, y_to] + gets[piece, SUM_UP + y_to].astype(jnp.float32)
                + gets[piece, OWN_DOWN - y_to].astype(jnp.float32))

    def cross(piece):
        for kind in (OWN_UP, OWN_DOWN, SUM_UP, SUM_DOWN):
            copy_of(kind, piece).wait_recv()
        sends[piece, ACROSS] = along_x(piece, 1 - y_pos).astype(jnp.bfloat16)
        copy_of(ACROSS, piece).start()
        mine[piece, y_pos] = along_x(piece, y_pos)

    def finish(piece):
        copy_of(ACROSS, piece).wait_recv()
        total = mine[piece, y_pos] + gets[piece, ACROSS].astype(jnp.float32)
        round_id = piece // 2
        scale = scale_ref[round_id]
        for half in range(2):
            for fine in range(FINE):
                block = total[fine * 8 : fine * 8 + 8, half * 128 : half * 128 + 128] * scale
                lag = ((piece % 2) * 2 + half) * FINE + fine
                at = pl.ds(pl.multiple_of(lag * 128, 128), 128)
                out_ref[round_id, :, at] = block.astype(jnp.bfloat16)

    pieces = ROUNDS * 2

    @pl.loop(0, pieces + 3)
    def _(step):
        @pl.when(step < pieces)
        def _():
            compute(step)

        @pl.when(jnp.logical_and(step >= 1, step < pieces + 1))
        def _():
            pass_on(step - 1)

        @pl.when(jnp.logical_and(step >= 2, step < pieces + 2))
        def _():
            cross(step - 2)

        @pl.when(step >= 3)
        def _():
            finish(step - 3)

    for copy in pair_copies:
        copy.wait_send()

    @pl.loop(0, pieces)
    def _(piece):
        for kind in range(7):
            copy_of(kind, piece).wait_send()


def stack(own, partners, scale):
    block_rows, two_bins = own.shape
    bins = two_bins // 2
    cosine, sine = tables(bins)
    rows = FINE * 8
    pieces = 4
    bf16, f32 = jnp.bfloat16, jnp.float32
    return pl.pallas_call(
        stack_kernel,
        name="stack",
        out_shape=jax.ShapeDtypeStruct((ROUNDS, 8, LAGS * block_rows), bf16),
        in_specs=[pl.BlockSpec(memory_space=pltpu.VMEM)] * 5,
        out_specs=pl.BlockSpec(memory_space=pltpu.VMEM),
        scratch_shapes=[
            pltpu.VMEM((block_rows, two_bins), bf16),
            pltpu.VMEM((ROUNDS, block_rows, two_bins), bf16),
            pltpu.VMEM((8 * rows, 2 * two_bins), bf16),
            pltpu.VMEM((ROUNDS * COARSE * block_rows, 2 * two_bins), bf16),
            pltpu.VMEM((pieces, 2, rows, 256), f32),
            pltpu.VMEM((pieces, 2, rows, 256), f32),
            pltpu.VMEM((pieces, 7, rows, 256), bf16),
            pltpu.VMEM((pieces, 7, rows, 256), bf16),
            pltpu.SemaphoreType.DMA((3,)),
            pltpu.SemaphoreType.DMA((3,)),
            pltpu.SemaphoreType.DMA((pieces, 7)),
            pltpu.SemaphoreType.DMA((pieces, 7)),
        ],
        compiler_params=pltpu.CompilerParams(
            collective_id=0, has_side_effects=True, vmem_limit_bytes=48 << 20),
    )(own, partners, jnp.asarray(cosine), jnp.asarray(sine), scale)


def partner_2(value, axis, apart):
    mask = 2**apart
    pairs = [(source, source ^ mask) for source in range(lax.axis_size(axis))]
    return lax.ppermute(value, axis, pairs)


def whiten(spectra, flags):
    values = spectra.astype(jnp.float32)
    mean_square = jnp.mean(values * values, axis=-1, keepdims=True)
    return (flags.astype(jnp.float32)[..., None] * values * lax.rsqrt(mean_square + 1e-06)).astype(
        jnp.bfloat16
    )


def deliver(values, flip_bits):
    levels = lax.axis_size("chan").bit_length() - 1
    first, second = values, values
    for bit_number in range(levels):
        taken = jnp.right_shift(flip_bits, bit_number) & 1 == 1
        moved = partner_2(jnp.where(taken, first, second), "chan", bit_number)
        first = jnp.where(taken, moved, first)
        second = jnp.where(taken, second, moved)
    return first, second


def shards(spectra, masks, matching):
    block_id = lax.axis_index("chan")
    slot_id = lax.axis_index("win")
    win_count = lax.axis_size("win")
    w_count, block_rows, two_bins = spectra.shape
    bin_count = two_bins // 2
    row_count = block_rows // win_count
    own_flags = lax.dynamic_slice(
        masks, (slot_id * w_count, block_id * block_rows), (w_count, block_rows)
    )
    whitened = whiten(spectra, own_flags)[0]
    flags = masks.astype(jnp.bfloat16)
    own_cols = lax.dynamic_slice_in_dim(
        flags, block_id * block_rows + slot_id * row_count, row_count, 1)
    scales = []
    for round_id in range(ROUNDS):
        partner = matching[round_id, block_id]
        other_cols = lax.dynamic_slice_in_dim(flags, partner * block_rows, block_rows, 1)
        counts = lax.dot_general(
            own_cols, other_cols, (((0,), (0,)), ((), ())), preferred_element_type=jnp.float32
        )
        scales.append(lax.rsqrt(bin_count * jnp.maximum(counts, 1.0)))
    first, second = deliver(whitened, jnp.bitwise_xor(matching[0, block_id], block_id))
    return stack(whitened, jnp.stack([first, second]), jnp.stack(scales))


def solution(mesh):
    in_specs = (P("win", "chan", None), P(), P())
    out_specs = P(None, ("chan", "win"), None)
    return jax.shard_map(shards, mesh=mesh, in_specs=in_specs, out_specs=out_specs, check_vma=False)
```

time: 393 us -> 142 us (0.36)
  waiting for transfers between devices: 214 us -> 63.4 us
  other arithmetic: 48.6 us -> 3 us
  Pallas kernels: 0 us -> 41.6 us
  local copies, waits for them, and re-layouts: 25.9 us -> 2.86 us
  starting transfers between devices: 49.1 us -> 26.9 us
  loops' own time: 20 us -> 0 us
  matrix products: 18.5 us -> 0.52 us
  between operations: 16.3 us -> 2.07 us
    reduce_scatter x2 -> x0, waiting for transfers between devices: 154 us -> none  [scattered(): lax.psum_scatter(everything.astype(jnp.bfloat16), axis, scatter_dimension...]
    pallas_call x0 -> x1, Pallas kernels: none -> 41.6 us  [stack(): pl.pallas_call(stack_kernel, name='stack', out_shape=jax.ShapeDtypeStruct...]
    sin x32 -> x0, other arithmetic: 25.8 us -> none  [tables(): return (jnp.cos(angle), jnp.sin(angle))]
    ppermute x9 -> x5, starting transfers between devices: 49.1 us -> 26.9 us  [partner_2(): return lax.ppermute(value, axis, pairs)]
    another operation x2 -> x0, loops' own time: 20 us -> none  [rows_term(): lax.map(one_piece, jnp.arange(row_total // row_step, dtype=jnp.int32))]
    dynamic_slice x33 -> x1, local copies, waits for them, and re-layouts: 19.6 us -> 0.65 us  [shards(): partner = matching[round_id, block_id]]
    dot_general x32 -> x0, matrix products: 18.1 us -> none  [one_piece(): lax.dot_general(rotated, other_spec, (((0, 2), (0, 2)), ((), ())), prefer...]
    another operation x35 -> x3, other arithmetic: 16 us -> 0.16 us  [shards(): return stack(whitened, jnp.stack([first, second]), jnp.stack(scales))]
  transfers between devices with their start and end apart: 11 -> 5, of which waited for: 8 -> 5; matrix products, arithmetic and copies ran while one was open for 21% -> 1% of each run, Pallas kernels for 0% -> 0%
where the time goes in v1:
time: 142 us; the launch traced here: 140 us
  waiting for transfers between devices  63.4 us (45%)
  Pallas kernels  41.6 us (29%)
  starting transfers between devices  26.9 us (19%)
  other arithmetic  3 us (2%)
  local copies, waits for them, and re-layouts  2.86 us (2%)
  between operations  2.07 us (1%)
    ppermute x5, waiting for transfers between devices, partner_2(): return lax.ppermute(value, axis, pairs)  63.4 us
    pallas_call x1, Pallas kernels, stack(): pl.pallas_call(stack_kernel, name='stack', out_shape=jax.ShapeDtypeStruct...  41.6 us
    ppermute x5, starting transfers between devices, partner_2(): return lax.ppermute(value, axis, pairs)  26.9 us
  transfers between devices with their start and end apart: 5, of which 5 were waited for; matrix products, arithmetic and copies ran while one was open for 1% of the time, Pallas kernels for 0%

profile of v1, /device:TPU:6, one launch (start us, length us, event | category | flops | bytes accessed | tf_op | source)
XLA Modules:
  0.0 140.4 jit_solution(13246873948189298390)
XLA Ops:
  0.0 1.2 fusion.8
  1.2 0.8 convert_bitcast_fusion
  2.0 0.0 copy-done.2
  2.0 0.2 fusion.9.own_ref
  2.2 3.5 %collective-permute-start = (bf16[128,1536]{1,0:T(8,128)(2,1)S(1)}, bf16[128,1536]{1,0:T(8,128)(2,1)S(1)}, u32[]{:S(2)}, u32[]{:S(2)}) collective-permute-start(bf16[128,1536]{1,0:T(8,128)(2,1)S(1)} %fusion.9.own_ref), channel_id=1, source_target_pairs={{0,16},{16,0},{32,48},{48,32},{64,80},{80,64},{96,112},{112,96},{1... | collective-permute-start | bytes 1179656 | tf_op jit(solution)/shard_map/ppermute | solution.py:225
  5.7 0.0 copy-start.4
  5.8 0.7 copy-done.4
  6.4 0.6 constant_dynamic-slice_fusion.1
  7.7 7.3 %collective-permute-done = bf16[128,1536]{1,0:T(8,128)(2,1)S(1)} collective-permute-done((bf16[128,1536]{1,0:T(8,128)(2,1)S(1)}, bf16[128,1536]{1,0:T(8,128)(2,1)S(1)}, u32[]{:S(2)}, u32[]{:S(2)}) %collective-permute-start) | collective-permute-done | bytes 393248 | tf_op jit(solution)/shard_map/ppermute | solution.py:225
  15.0 0.4 broadcast_select_fusion.4
  15.4 4.5 %collective-permute-start.1 = (bf16[128,1536]{1,0:T(8,128)(2,1)S(1)}, bf16[128,1536]{1,0:T(8,128)(2,1)S(1)}, u32[]{:S(2)}, u32[]{:S(2)}) collective-permute-start(bf16[128,1536]{1,0:T(8,128)(2,1)S(1)} %get-tuple-element.8), channel_id=1, source_target_pairs={{0,32},{16,48},{32,0},{48,16},{64,96},{80,112},{96,64},{112,80},{1... | collective-permute-start | bytes 1179656 | tf_op jit(solution)/shard_map/ppermute | solution.py:225
  19.9 16.7 %collective-permute-done.1 = bf16[128,1536]{1,0:T(8,128)(2,1)S(1)} collective-permute-done((bf16[128,1536]{1,0:T(8,128)(2,1)S(1)}, bf16[128,1536]{1,0:T(8,128)(2,1)S(1)}, u32[]{:S(2)}, u32[]{:S(2)}) %collective-permute-start.1) | collective-permute-done | bytes 393248 | tf_op jit(solution)/shard_map/ppermute | solution.py:225
  36.6 0.1 broadcast_select_fusion.7
  36.7 4.3 %collective-permute-start.2 = (bf16[128,1536]{1,0:T(8,128)(2,1)S(1)}, bf16[128,1536]{1,0:T(8,128)(2,1)S(1)}, u32[]{:S(2)}, u32[]{:S(2)}) collective-permute-start(bf16[128,1536]{1,0:T(8,128)(2,1)S(1)} %broadcast_select_fusion.7), channel_id=1, source_target_pairs={{0,64},{16,80},{32,96},{48,112},{64,0},{80,16},{96,32},{112,48},{1... | collective-permute-start | bytes 1179656 | tf_op jit(solution)/shard_map/ppermute | solution.py:225
  41.0 8.3 %collective-permute-done.2 = bf16[128,1536]{1,0:T(8,128)(2,1)S(1)} collective-permute-done((bf16[128,1536]{1,0:T(8,128)(2,1)S(1)}, bf16[128,1536]{1,0:T(8,128)(2,1)S(1)}, u32[]{:S(2)}, u32[]{:S(2)}) %collective-permute-start.2) | collective-permute-done | bytes 393248 | tf_op jit(solution)/shard_map/ppermute | solution.py:225
  49.2 0.1 broadcast_select_fusion.10
  49.3 6.1 %collective-permute-start.3 = (bf16[128,1536]{1,0:T(8,128)(2,1)S(1)}, bf16[128,1536]{1,0:T(8,128)(2,1)S(1)}, u32[]{:S(2)}, u32[]{:S(2)}) collective-permute-start(bf16[128,1536]{1,0:T(8,128)(2,1)S(1)} %get-tuple-element.5), channel_id=1, source_target_pairs={{0,128},{16,144},{32,160},{48,176},{64,192},{80,208},{96,224},{112... | collective-permute-start | bytes 1179656 | tf_op jit(solution)/shard_map/ppermute | solution.py:225
  55.4 16.1 %collective-permute-done.3 = bf16[128,1536]{1,0:T(8,128)(2,1)S(1)} collective-permute-done((bf16[128,1536]{1,0:T(8,128)(2,1)S(1)}, bf16[128,1536]{1,0:T(8,128)(2,1)S(1)}, u32[]{:S(2)}, u32[]{:S(2)}) %collective-permute-start.3) | collective-permute-done | bytes 393248 | tf_op jit(solution)/shard_map/ppermute | solution.py:225
  71.5 0.1 broadcast_select_fusion.11
  71.6 8.6 %collective-permute-start.4 = (bf16[128,1536]{1,0:T(8,128)(2,1)S(1)}, bf16[128,1536]{1,0:T(8,128)(2,1)S(1)}, u32[]{:S(2)}, u32[]{:S(2)}) collective-permute-start(bf16[128,1536]{1,0:T(8,128)(2,1)S(1)} %broadcast_select_fusion.11), channel_id=1, source_target_pairs={{0,256},{16,272},{32,288},{48,304},{64,320},{80,336},{96,352},{112... | collective-permute-start | bytes 1179656 | tf_op jit(solution)/shard_map/ppermute | solution.py:225
  80.8 0.0 copy-done.3
  81.5 0.3 fusion.5
  81.8 0.3 fusion.2
  82.0 15.0 %collective-permute-done.4 = bf16[128,1536]{1,0:T(8,128)(2,1)S(1)} collective-permute-done((bf16[128,1536]{1,0:T(8,128)(2,1)S(1)}, bf16[128,1536]{1,0:T(8,128)(2,1)S(1)}, u32[]{:S(2)}, u32[]{:S(2)}) %collective-permute-start.4) | collective-permute-done | bytes 393248 | tf_op jit(solution)/shard_map/ppermute | solution.py:225
  97.1 0.1 select_bitcast_fusion.1
  97.2 0.0 copy-start
  97.2 0.0 copy-start.1
  97.2 0.1 pad_maximum_fusion.part_ref
  97.3 0.8 copy-done
  98.0 0.0 copy-done.1
  98.1 41.6 %stack.25 = bf16[2,8,8192]{2,1,0:T(8,128)(2,1)S(1)} custom-call(bf16[128,1536]{1,0:T(8,128)(2,1)S(1)} %fusion.9.own_ref, bf16[2,128,1536]{2,1,0:T(8,128)(2,1)S(1)} %pad_maximum_fusion.part_ref, f32[20,768]{1,0:T(8,128)S(1)} %copy-done, f32[20,768]{1,0:T(8,128)S(1)} %copy-done.1, f32[2,8,128]{2,1,0:T(8,128)S(1)} %pad_maximum_fusion.1.scale_ref), custom_call_target="tpu_custom_call" | custom-call | tf_op jit(solution)/shard_map/stack/pallas_call | solution.py:197
  139.7 0.7 copy.7
  (5 shorter events, 0.0 us)
Async XLA Ops:
  0.0 2.0 %copy-start.2 = (bf16[1,128,1536]{2,1,0:T(8,128)(2,1)S(1)}, bf16[1,128,1536]{2,1,0:T(8,128)(2,1)}, u32[]{:S(2)}) copy-start(bf16[1,128,1536]{2,1,0:T(8,128)(2,1)} %param.5) | copy-start | bytes 1179652
  2.2 12.7 %collective-permute-start = (bf16[128,1536]{1,0:T(8,128)(2,1)S(1)}, bf16[128,1536]{1,0:T(8,128)(2,1)S(1)}, u32[]{:S(2)}, u32[]{:S(2)}) collective-permute-start(bf16[128,1536]{1,0:T(8,128)(2,1)S(1)} %fusion.9.own_ref), channel_id=1, source_target_pairs={{0,16},{16,0},{32,48},{48,32},{64,80},{80,64},{96,112},{112,96},{1... | collective-permute-start | bytes 1179656 | tf_op jit(solution)/shard_map/ppermute | solution.py:225
  5.7 0.7 copy-start.4
  15.4 21.2 %collective-permute-start.1 = (bf16[128,1536]{1,0:T(8,128)(2,1)S(1)}, bf16[128,1536]{1,0:T(8,128)(2,1)S(1)}, u32[]{:S(2)}, u32[]{:S(2)}) collective-permute-start(bf16[128,1536]{1,0:T(8,128)(2,1)S(1)} %get-tuple-element.8), channel_id=1, source_target_pairs={{0,32},{16,48},{32,0},{48,16},{64,96},{80,112},{96,64},{112,80},{1... | collective-permute-start | bytes 1179656 | tf_op jit(solution)/shard_map/ppermute | solution.py:225
  36.7 12.6 %collective-permute-start.2 = (bf16[128,1536]{1,0:T(8,128)(2,1)S(1)}, bf16[128,1536]{1,0:T(8,128)(2,1)S(1)}, u32[]{:S(2)}, u32[]{:S(2)}) collective-permute-start(bf16[128,1536]{1,0:T(8,128)(2,1)S(1)} %broadcast_select_fusion.7), channel_id=1, source_target_pairs={{0,64},{16,80},{32,96},{48,112},{64,0},{80,16},{96,32},{112,48},{1... | collective-permute-start | bytes 1179656 | tf_op jit(solution)/shard_map/ppermute | solution.py:225
  49.3 22.2 %collective-permute-start.3 = (bf16[128,1536]{1,0:T(8,128)(2,1)S(1)}, bf16[128,1536]{1,0:T(8,128)(2,1)S(1)}, u32[]{:S(2)}, u32[]{:S(2)}) collective-permute-start(bf16[128,1536]{1,0:T(8,128)(2,1)S(1)} %get-tuple-element.5), channel_id=1, source_target_pairs={{0,128},{16,144},{32,160},{48,176},{64,192},{80,208},{96,224},{112... | collective-permute-start | bytes 1179656 | tf_op jit(solution)/shard_map/ppermute | solution.py:225
  71.5 9.3 %copy-start.3 = (s32[16,4096]{1,0:T(8,128)S(1)}, s32[16,4096]{1,0:T(8,128)}, u32[]{:S(2)}) copy-start(s32[16,4096]{1,0:T(8,128)} %param.6) | copy-start | bytes 786436
  71.6 25.5 %collective-permute-start.4 = (bf16[128,1536]{1,0:T(8,128)(2,1)S(1)}, bf16[128,1536]{1,0:T(8,128)(2,1)S(1)}, u32[]{:S(2)}, u32[]{:S(2)}) collective-permute-start(bf16[128,1536]{1,0:T(8,128)(2,1)S(1)} %broadcast_select_fusion.11), channel_id=1, source_target_pairs={{0,256},{16,272},{32,288},{48,304},{64,320},{80,336},{96,352},{112... | collective-permute-start | bytes 1179656 | tf_op jit(solution)/shard_map/ppermute | solution.py:225
  97.2 0.9 copy-start
  97.2 0.9 copy-start.1
